TPU v7x, 32 devices: a whole 2x2x4 slice. The times are simulated.
32 devices in a mesh: gx: 8 (over z, y), gy: 4 (over x, core).
Axes of the slice: x: 2, y: 2, z: 4, core: 2. Of those that a mesh axis runs over, the one named last changes fastest.
Arguments:
- vorticity_grid: float32 [4096, 4096], P(('gx', 'gy')), may hold values from -6 to 6
- forcing_grid: float32 [4096, 4096], P(('gx', 'gy')), may hold values from -12 to 12
- cutoff: int32 [1], replicated, may hold values from 853 to 1365
- forcing_shells: int32 [4], replicated, may hold values from 2 to 127
Outputs:
- lifted_spectrum: float32 [2, 4096, 4096], P(None, ('gx', 'gy'))
- coarse_field: float32 [256, 256], P(('gx', 'gy'))
Inputs may be any that keep to these rules, and one draw needn't show every extreme that they name: Nonlinear modes with an absolute wavenumber index above cutoff are removed.
All inputs are finite; a program needn't handle non-finite values.
Results may differ from a plain program's by a relative error of at most 0.0001.
Values sent between devices are 32-bit elements; how exact they have to be, the bound alone decides.
A program may use at most 128 MiB of HBM per device.

v0:
```python
import math
import jax
import jax.numpy as jnp
from jax import lax
from jax.sharding import PartitionSpec as P

RADIX = 64
LOW = 256
SHELLS = 4
time_step = 0.05
viscosity = 0.05
coarse_ratio = 4.0


def signed_index(index_array, length_of):
    return jnp.where(index_array < length_of // 2, index_array, index_array - length_of)


def pair_tables(first_ids, second_ids, length_of):
    product = first_ids[:, None] * second_ids[None, :] % length_of
    phases = 2.0 * math.pi / length_of * product.astype(jnp.float32)
    factor = 1.0 / math.sqrt(length_of)
    return (jnp.cos(phases) * factor, jnp.sin(phases) * factor)


def contract(pattern, left_side, right_side):
    return jnp.einsum(pattern, left_side, right_side, precision=lax.Precision.HIGHEST)


def complex_table(direction):
    indices = jnp.arange(RADIX, dtype=jnp.int32)
    cos_table, sin_table = pair_tables(indices, indices, RADIX)
    signed_sin = direction * sin_table
    from_real = jnp.stack([cos_table, signed_sin], axis=1)
    from_imag = jnp.stack([-signed_sin, cos_table], axis=1)
    return jnp.stack([from_real, from_imag], axis=0)


def dft_last(values, direction, is_real):
    length_of = values.shape[-1]
    table = complex_table(direction)
    if is_real:
        leading = values.shape[:-1]
        split_values = values.reshape(leading + (RADIX, RADIX))
        first = contract("...ab,adk->d...kb", split_values, table[0])
    else:
        leading = values.shape[1:-1]
        split_values = values.reshape((2,) + leading + (RADIX, RADIX))
        first = contract("c...ab,cadk->d...kb", split_values, table)
    indices = jnp.arange(RADIX, dtype=jnp.int32)
    twiddle_index = indices[:, None] * indices[None, :] % length_of
    twiddle_phase = 2.0 * math.pi / length_of * twiddle_index.astype(jnp.float32)
    twiddle_real = jnp.cos(twiddle_phase)
    twiddle_imag = direction * jnp.sin(twiddle_phase)
    turned = jnp.stack(
        [
            first[0] * twiddle_real - first[1] * twiddle_imag,
            first[0] * twiddle_imag + first[1] * twiddle_real,
        ]
    )
    final = contract("c...kb,cbdj->d...jk", turned, table)
    return final.reshape((2,) + leading + (length_of,))


def rows_to_grid(packed):
    return lax.all_to_all(packed, ("gx", "gy"), split_axis=1, concat_axis=2, tiled=True)


def rows_to_waves(packed):
    return lax.all_to_all(packed, ("gx", "gy"), split_axis=2, concat_axis=1, tiled=True)


def forward(fields):
    field_count = fields.shape[0]
    half = dft_last(fields, -1.0, True)
    moved = rows_to_waves(half.reshape((2 * field_count,) + half.shape[2:]))
    moved = jnp.swapaxes(moved, 1, 2)
    return dft_last(moved.reshape((2, field_count) + moved.shape[1:]), -1.0, False)


def inverse(spectra):
    field_count = spectra.shape[1]
    half = dft_last(spectra, 1.0, False)
    packed = jnp.swapaxes(half.reshape((2 * field_count,) + half.shape[2:]), 1, 2)
    moved = rows_to_grid(packed)
    return dft_last(moved.reshape((2, field_count) + moved.shape[1:]), 1.0, False)


def body(vorticity_grid, forcing_grid, cutoff, forcing_shells):
    row_count = vorticity_grid.shape[0]
    grid_size = vorticity_grid.shape[1]
    device_rank = lax.axis_index("gx") * lax.axis_size("gy") + lax.axis_index("gy")
    device_total = lax.axis_size("gx") * lax.axis_size("gy")
    row_start = device_rank * row_count
    row_ids = row_start + jnp.arange(row_count, dtype=jnp.int32)
    col_ids = jnp.arange(grid_size, dtype=jnp.int32)
    wave_y = signed_index(row_ids, grid_size)[:, None]
    wave_x = signed_index(col_ids, grid_size)[None, :]
    wave_unit = 2.0 * math.pi / grid_size
    deriv_y = (
        jnp.where(row_ids[:, None] == grid_size // 2, 0, wave_y).astype(jnp.float32) * wave_unit
    )
    deriv_x = (
        jnp.where(col_ids[None, :] == grid_size // 2, 0, wave_x).astype(jnp.float32) * wave_unit
    )
    squares = wave_x * wave_x + wave_y * wave_y
    laplace = squares.astype(jnp.float32) * (wave_unit * wave_unit)
    inverse_lap = jnp.where(squares == 0, 0.0, 1.0 / jnp.maximum(laplace, wave_unit * wave_unit))
    dealias = (jnp.abs(wave_x) <= cutoff[0]) & (jnp.abs(wave_y) <= cutoff[0])
    shell_mask = jnp.zeros((row_count, grid_size), dtype=bool)
    for shell_index in range(SHELLS):
        radius = forcing_shells[shell_index]
        shell_mask = shell_mask | (radius * radius <= squares) & (
            squares < (radius + 1) * (radius + 1)
        )
    started = forward(jnp.stack([vorticity_grid, forcing_grid]))
    drive_real = jnp.where(shell_mask, started[0, 1], 0.0)
    drive_imag = jnp.where(shell_mask, started[1, 1], 0.0)
    state_real = started[0, 0]
    state_imag = started[1, 0]

    def tendency(now_real, now_imag):
        stream_real = now_real * inverse_lap
        stream_imag = now_imag * inverse_lap
        speed_real = deriv_x * stream_real - deriv_y * stream_imag
        speed_imag = deriv_x * stream_imag + deriv_y * stream_real
        slope_real = -deriv_y * now_real - deriv_x * now_imag
        slope_imag = -deriv_y * now_imag + deriv_x * now_real
        spectra = jnp.stack(
            [jnp.stack([speed_real, slope_real]), jnp.stack([speed_imag, slope_imag])]
        )
        grids = inverse(spectra)
        advect = grids[0, 0] * grids[0, 1] + grids[1, 0] * grids[1, 1]
        term = forward(advect[None])
        out_real = (
            -jnp.where(dealias, term[0, 0], 0.0) - viscosity * laplace * now_real + drive_real
        )
        out_imag = (
            -jnp.where(dealias, term[1, 0], 0.0) - viscosity * laplace * now_imag + drive_imag
        )
        return (out_real, out_imag)

    earlier_real = state_real
    earlier_imag = state_imag
    first_real, first_imag = tendency(state_real, state_imag)
    second_real, second_imag = tendency(
        state_real + time_step * first_real, state_imag + time_step * first_imag
    )
    state_real = state_real + 0.5 * time_step * (first_real + second_real)
    state_imag = state_imag + 0.5 * time_step * (first_imag + second_imag)
    projected_real = state_real + coarse_ratio * (state_real - earlier_real)
    projected_imag = state_imag + coarse_ratio * (state_imag - earlier_imag)
    half_low = LOW // 2
    low_modes = (
        (wave_x >= -half_low) & (wave_x < half_low) & (wave_y >= -half_low) & (wave_y < half_low)
    )
    lifted_real = jnp.where(low_modes, projected_real, state_real)
    lifted_imag = jnp.where(low_modes, projected_imag, state_imag)
    projected = jnp.stack([projected_real, projected_imag])
    low_columns = jnp.concatenate(
        [projected[:, :, :half_low], projected[:, :, grid_size - half_low :]], axis=2
    )
    block_ids = jnp.arange(LOW, dtype=jnp.int32)
    coarse_rows = LOW // device_total
    every_row = lax.all_gather(low_columns, ("gx", "gy"), axis=1, tiled=True)
    block_low = jnp.concatenate(
        [every_row[:, :half_low], every_row[:, grid_size - half_low :]], axis=1
    )
    own_ids = device_rank * coarse_rows + jnp.arange(coarse_rows, dtype=jnp.int32)
    column_cos, column_sin = pair_tables(block_ids, own_ids, LOW)
    mixed_real = contract("qp,pa->qa", block_low[0], column_cos) - contract(
        "qp,pa->qa", block_low[1], column_sin
    )
    mixed_imag = contract("qp,pa->qa", block_low[0], column_sin) + contract(
        "qp,pa->qa", block_low[1], column_cos
    )
    row_cos, row_sin = pair_tables(block_ids, block_ids, LOW)
    coarse = contract("qa,qb->ab", mixed_real, row_cos) - contract("qa,qb->ab", mixed_imag, row_sin)
    return (jnp.stack([lifted_real, lifted_imag]), coarse)


def solution(mesh):
    placed = (P(("gx", "gy"), None), P(("gx", "gy"), None), P(), P())
    return jax.shard_map(
        body,
        mesh=mesh,
        in_specs=placed,
        out_specs=(P(None, ("gx", "gy"), None), P(("gx", "gy"), None)),
        check_vma=False,
    )
```

profile of v0, /device:TPU:0, one launch (start us, length us, event | category | flops | bytes accessed | tf_op | source)
XLA Modules:
  0.0 1329.7 jit_solution(10226126901157418966)
XLA Ops:
  9.7 2.5 copy.174
  15.7 6.7 fusion.61
  26.6 12.5 fusion.62
  39.1 4.9 copy.178
  44.0 18.6 %copy.179 = f32[4,128,4096]{1,0,2:T(4,128)} copy(f32[4,128,4096]{1,2,0:T(8,128)S(1)} %bitcast.399) | data formatting | bytes 16777216 | tf_op jit(solution)/shard_map/reshape;reshape | solution.py:76
  62.6 7.9 all-to-all-start
  70.7 185.6 %all-to-all-done = f32[4,128,4096]{1,0,2:T(4,128)} async-done(((f32[4,128,4096]{1,0,2:T(4,128)}), f32[4,128,4096]{1,0,2:T(4,128)}, u32[]{:S(2)}, u32[]{:S(2)}) %all-to-all-start) | async-done | bytes 8388640 | tf_op jit(solution)/shard_map/all_to_all | solution.py:70
  256.3 7.2 copy.180
  263.5 9.0 copy.181
  272.4 15.8 %fusion.65 = f32[2,2,128,64,64]{2,3,4,1,0:T(8,128)S(1)} fusion(f32[2,2,128,64,64]{2,4,3,1,0:T(8,128)} %bitcast.401, f32[2,64,2,64,1,1]{1,3,2,0,5,4:T(8,128)S(1)} %get-tuple-element.58), kind=kOutput, calls=%fused_computation.112 | convolution fusion | flops 3221225472 | bytes 16842752 | tf_op jit(solution)/shard_map/c...ab,cadk->d...kb/dot_general | solution.py:27
  291.7 12.5 fusion.68
  304.2 4.9 copy.186
  309.1 2.8 fusion.314
  313.6 5.1 multiply_subtract_fusion.13
  318.7 8.5 fusion.90
  330.7 12.7 fusion.71
  343.4 4.9 copy.196
  348.3 17.8 %copy.197 = f32[4,4096,128]{2,0,1:T(4,128)S(1)} copy(f32[4,4096,128]{2,1,0:T(8,128)S(1)} %bitcast.402) | data formatting | bytes 16777216 | tf_op jit(solution)/shard_map/transpose | solution.py:84
  366.1 185.3 %all_to_all.84 = f32[4,4096,128]{2,0,1:T(4,128)S(1)} all-to-all(f32[4,4096,128]{2,0,1:T(4,128)S(1)} %copy.197), channel_id=1, replica_groups=mesh['gx'=8,'gy'=4] {'gx','gy'}, dimensions={1} | all-to-all | bytes 16777216 | tf_op jit(solution)/shard_map/all_to_all | solution.py:66
  551.4 3.8 copy.198
  555.2 9.0 copy.199
  564.1 15.8 %fusion.74 = f32[2,2,128,64,64]{2,3,4,1,0:T(8,128)S(1)} fusion(f32[2,2,128,64,64]{2,4,3,1,0:T(8,128)} %bitcast.404, f32[1,64,2,64]{1,3,2,0:T(8,128)S(1)} %get-tuple-element.60, f32[1,64,2,64]{1,3,2,0:T(8,128)S(1)} %get-tuple-element.59), kind=kOutput, calls=%fused_computation.115 | convolution fusion | flops 3221241856 | bytes 16842752 | tf_op jit(solution)/shard_map/c...ab,cadk->d...kb/dot_general | solution.py:27
  583.4 12.5 fusion.77
  595.9 4.9 copy.204
  601.2 4.6 convolution_bitcast_fusion.1
  608.2 5.9 fusion.95
  614.1 2.4 copy.208
  616.5 16.1 %copy.209 = f32[2,128,4096]{1,0,2:T(2,128)} copy(f32[2,128,4096]{1,2,0:T(8,128)S(1)} %bitcast.412) | data formatting | bytes 8388608 | tf_op jit(solution)/shard_map/reshape;reshape | solution.py:76
  632.7 4.0 all-to-all-start.2
  645.7 84.6 %all-to-all-done.2 = f32[2,128,4096]{1,0,2:T(2,128)} async-done(((f32[2,128,4096]{1,0,2:T(2,128)}), f32[2,128,4096]{1,0,2:T(2,128)}, u32[]{:S(2)}, u32[]{:S(2)}) %all-to-all-start.2) | async-done | bytes 4194336 | tf_op jit(solution)/shard_map/all_to_all | solution.py:70
  730.3 4.5 copy.210
  734.8 5.7 copy.211
  740.5 8.4 fusion.98
  751.2 6.1 fusion.101
  757.3 10.4 multiply_subtract_fusion.9
  769.3 8.5 fusion.89
  777.9 2.1 multiply_subtract_fusion.1
  781.6 12.5 fusion.80
  794.1 4.9 copy.227
  799.0 17.8 %copy.228 = f32[4,4096,128]{2,0,1:T(4,128)S(1)} copy(f32[4,4096,128]{2,1,0:T(8,128)S(1)} %bitcast.405) | data formatting | bytes 16777216 | tf_op jit(solution)/shard_map/transpose | solution.py:84
  816.8 187.4 %all_to_all.85 = f32[4,4096,128]{2,0,1:T(4,128)S(1)} all-to-all(f32[4,4096,128]{2,0,1:T(4,128)S(1)} %copy.228), channel_id=1, replica_groups=mesh['gx'=8,'gy'=4] {'gx','gy'}, dimensions={1} | all-to-all | bytes 16777216 | tf_op jit(solution)/shard_map/all_to_all | solution.py:66
  1004.2 3.8 copy.229
  1008.0 9.0 copy.230
  1017.0 15.8 %fusion.83 = f32[2,2,128,64,64]{2,3,4,1,0:T(8,128)S(1)} fusion(f32[2,2,128,64,64]{2,4,3,1,0:T(8,128)} %bitcast.407, f32[1,64,2,64]{1,3,2,0:T(8,128)S(1)} %get-tuple-element.60, f32[1,64,2,64]{1,3,2,0:T(8,128)S(1)} %get-tuple-element.59), kind=kOutput, calls=%fused_computation.118 | convolution fusion | flops 3221241856 | bytes 16842752 | tf_op jit(solution)/shard_map/c...ab,cadk->d...kb/dot_general | solution.py:27
  1036.5 12.5 fusion.86
  1049.0 4.9 copy.235
  1054.2 4.6 convolution_bitcast_fusion
  1061.1 5.9 fusion.104
  1066.9 2.4 copy.239
  1069.4 16.5 %copy.240 = f32[2,128,4096]{1,0,2:T(2,128)} copy(f32[2,128,4096]{1,2,0:T(8,128)S(1)} %bitcast.415) | data formatting | bytes 8388608 | tf_op jit(solution)/shard_map/reshape;reshape | solution.py:76
  1085.9 3.9 all-to-all-start.4
  1089.9 2.5 fusion.315
  1092.4 2.5 copy.248
  1096.2 87.3 %all-to-all-done.4 = f32[2,128,4096]{1,0,2:T(2,128)} async-done(((f32[2,128,4096]{1,0,2:T(2,128)}), f32[2,128,4096]{1,0,2:T(2,128)}, u32[]{:S(2)}, u32[]{:S(2)}) %all-to-all-start.4) | async-done | bytes 4194336 | tf_op jit(solution)/shard_map/all_to_all | solution.py:70
  1183.5 4.5 copy.241
  1188.0 5.7 copy.242
  1193.6 8.4 fusion.107
  1204.2 5.9 fusion.110
  1214.3 5.4 fusion.152
  1219.7 5.3 fusion.156
  1226.7 4.5 fusion.174
  1231.2 2.2 pad_maximum_fusion.6
  1233.4 5.8 copy.250
  1239.2 75.9 %all-gather.2.cloned.1.call-done = f32[2,4096,256]{1,2,0:T(8,128)} async-done(((f32[2,128,256]{1,2,0:T(8,128)}), f32[2,4096,256]{1,2,0:T(8,128)}) %all-gather.2.cloned.1.call-update) | async-done | bytes 8388624 | tf_op jit(solution)/shard_map/all_gather | solution.py:165
  (85 shorter events, 54.3 us)
Async XLA Ops:
  14.1 1.6 copy-start.5
  62.6 193.7 %all-to-all-start = ((f32[4,128,4096]{1,0,2:T(4,128)}), f32[4,128,4096]{1,0,2:T(4,128)}, u32[]{:S(2)}, u32[]{:S(2)}) async-start(f32[4,128,4096]{1,0,2:T(4,128)} %copy.179), calls=%async_computation | async-start | bytes 16777216 | tf_op jit(solution)/shard_map/all_to_all | solution.py:70
  309.1 4.5 copy-start
  313.6 5.1 copy-start.2
  632.7 4.0 copy-start.10
  632.7 97.7 %all-to-all-start.2 = ((f32[2,128,4096]{1,0,2:T(2,128)}), f32[2,128,4096]{1,0,2:T(2,128)}, u32[]{:S(2)}, u32[]{:S(2)}) async-start(f32[2,128,4096]{1,0,2:T(2,128)} %copy.209), calls=%async_computation.2 | async-start | bytes 8388608 | tf_op jit(solution)/shard_map/all_to_all | solution.py:70
  750.3 0.9 copy-start.9
  751.2 6.1 copy-start.3
  751.2 6.1 copy-start.6
  751.2 6.1 copy-start.7
  757.3 10.4 copy-start.1
  1085.9 97.6 %all-to-all-start.4 = ((f32[2,128,4096]{1,0,2:T(2,128)}), f32[2,128,4096]{1,0,2:T(2,128)}, u32[]{:S(2)}, u32[]{:S(2)}) async-start(f32[2,128,4096]{1,0,2:T(2,128)} %copy.240), calls=%async_computation.4 | async-start | bytes 8388608 | tf_op jit(solution)/shard_map/all_to_all | solution.py:70
  1089.8 225.3 %all-gather.2.cloned.1.call-start = ((), (), s32[]{:S(2)}) async-start(), calls=%async_computation.5 | async-start | bytes 8650752 | tf_op jit(solution)/shard_map/all_gather | solution.py:165
  1210.1 3.1 slice-start
  1210.7 3.0 slice-start.1
  1211.9 2.4 copy-start.4
  1225.0 1.7 copy-start.8
Sparse Core Ops, SparseCore 0:
  1225.9 89.2 all-gather.1
where the time goes:
time: 1340 us; the launch traced here: 1330 us
  waiting for transfers between devices  434 us (32%)
  blocking collectives  373 us (28%)
  local copies, waits for them, and re-layouts  214 us (16%)
  matrix products  202 us (15%)
  other arithmetic  67.4 us (5%)
  between operations  23.3 us (2%)
  starting transfers between devices  15.8 us (1%)
    all_to_all x2, blocking collectives, rows_to_grid(): lax.all_to_all(packed, ('gx', 'gy'), split_axis=1, concat_axis=2, tiled=T...  373 us
    all_to_all x3, waiting for transfers between devices, rows_to_waves(): lax.all_to_all(packed, ('gx', 'gy'), split_axis=2, concat_axis=1, tiled=T...  358 us
    dot_general x26, matrix products, contract(): jnp.einsum(pattern, left_side, right_side, precision=lax.Precision.HIGHEST)  202 us
    all_gather x1, waiting for transfers between devices, body(): every_row = lax.all_gather(low_columns, ('gx', 'gy'), axis=1, tiled=True)  75.9 us
    another operation x3, local copies, waits for them, and re-layouts, forward(): moved = rows_to_waves(half.reshape((2 * field_count,) + half.shape[2:]))  51.3 us
    all_to_all x6, local copies, waits for them, and re-layouts, rows_to_waves(): lax.all_to_all(packed, ('gx', 'gy'), split_axis=2, concat_axis=1, tiled=T...  36.4 us
    transpose x2, local copies, waits for them, and re-layouts, inverse(): jnp.swapaxes(half.reshape((2 * field_count,) + half.shape[2:]), 1, 2)  35.6 us
    transpose x8, local copies, waits for them, and re-layouts, contract(): jnp.einsum(pattern, left_side, right_side, precision=lax.Precision.HIGHEST)  34 us
  transfers between devices with their start and end apart: 4, of which 4 were waited for; matrix products, arithmetic and copies ran while one was open for 1% of the time, Pallas kernels for 0%

commit v1 on v0

--- a/solution.py
+++ b/solution.py
@@ -63,7 +63,12 @@
 
 
 def rows_to_grid(packed):
-    return lax.all_to_all(packed, ("gx", "gy"), split_axis=1, concat_axis=2, tiled=True)
+    return jnp.concatenate(
+        lax.all_to_all(
+            jnp.stack(jnp.split(packed, lax.axis_size(("gx", "gy")), axis=1)), ("gx", "gy"), 0, 0
+        ),
+        axis=2,
+    )
 
 
 def rows_to_waves(packed):

time: 1340 us -> 1300 us (0.970)
  local copies, waits for them, and re-layouts: 214 us -> 173 us
    transpose x2 -> x0, local copies, waits for them, and re-layouts: 35.6 us -> none  [inverse(): jnp.swapaxes(half.reshape((2 * field_count,) + half.shape[2:]), 1, 2)]
    all_to_all x4 -> x0, local copies, waits for them, and re-layouts: 25.5 us -> none  [rows_to_grid(): lax.all_to_all(packed, ('gx', 'gy'), split_axis=1, concat_axis=2, tiled=T...]
    reshape x0 -> x2, local copies, waits for them, and re-layouts: none -> 17.9 us  [rows_to_grid(): jnp.concatenate(lax.all_to_all(jnp.stack(jnp.split(packed, lax.axis_size(...]
  transfers between devices with their start and end apart: 4 -> 4, of which waited for: 4 -> 4; matrix products, arithmetic and copies ran while one was open for 1% -> 2% of each run, Pallas kernels for 0% -> 0%
where the time goes in v1:
time: 1300 us; the launch traced here: 1290 us
  waiting for transfers between devices  434 us (33%)
  blocking collectives  374 us (29%)
  matrix products  202 us (16%)
  local copies, waits for them, and re-layouts  173 us (13%)
  other arithmetic  67.4 us (5%)
  between operations  23.8 us (2%)
  starting transfers between devices  15.7 us (1%)
    all_to_all x2, blocking collectives, rows_to_grid(): lax.all_to_all(jnp.stack(jnp.split(packed, lax.axis_size(('gx', 'gy')), a...  374 us
    all_to_all x3, waiting for transfers between devices, rows_to_waves(): lax.all_to_all(packed, ('gx', 'gy'), split_axis=2, concat_axis=1, tiled=T...  358 us
    dot_general x26, matrix products, contract(): jnp.einsum(pattern, left_side, right_side, precision=lax.Precision.HIGHEST)  202 us
    all_gather x1, waiting for transfers between devices, body(): every_row = lax.all_gather(low_columns, ('gx', 'gy'), axis=1, tiled=True)  75.9 us
    another operation x3, local copies, waits for them, and re-layouts, forward(): moved = rows_to_waves(half.reshape((2 * field_count,) + half.shape[2:]))  51.3 us
    all_to_all x6, local copies, waits for them, and re-layouts, rows_to_waves(): lax.all_to_all(packed, ('gx', 'gy'), split_axis=2, concat_axis=1, tiled=T...  36.4 us
    transpose x8, local copies, waits for them, and re-layouts, contract(): jnp.einsum(pattern, left_side, right_side, precision=lax.Precision.HIGHEST)  34 us
  transfers between devices with their start and end apart: 4, of which 4 were waited for; matrix products, arithmetic and copies ran while one was open for 2% of the time, Pallas kernels for 0%

profile of v1, /device:TPU:0, one launch (start us, length us, event | category | flops | bytes accessed | tf_op | source)
XLA Modules:
  0.0 1289.1 jit_solution(298726615774462657)
XLA Ops:
  7.8 1.9 copy.172
  9.7 2.5 copy.174
  12.2 1.9 copy.173
  15.7 6.7 fusion.61
  26.6 12.5 fusion.62
  39.1 4.9 copy.178
  44.0 18.6 %copy.179 = f32[4,128,4096]{1,0,2:T(4,128)} copy(f32[4,128,4096]{1,2,0:T(8,128)S(1)} %bitcast.715) | data formatting | bytes 16777216 | tf_op jit(solution)/shard_map/reshape;reshape | solution.py:81
  62.6 7.9 all-to-all-start
  70.7 185.6 %all-to-all-done = f32[4,128,4096]{1,0,2:T(4,128)} async-done(((f32[4,128,4096]{1,0,2:T(4,128)}), f32[4,128,4096]{1,0,2:T(4,128)}, u32[]{:S(2)}, u32[]{:S(2)}) %all-to-all-start) | async-done | bytes 8388640 | tf_op jit(solution)/shard_map/all_to_all | solution.py:75
  256.3 7.2 copy.180
  263.5 9.0 copy.181
  272.4 15.8 %fusion.65 = f32[2,2,128,64,64]{2,3,4,1,0:T(8,128)S(1)} fusion(f32[2,2,128,64,64]{2,4,3,1,0:T(8,128)} %bitcast.717, f32[2,64,2,64,1,1]{1,3,2,0,5,4:T(8,128)S(1)} %get-tuple-element.58), kind=kOutput, calls=%fused_computation.112 | convolution fusion | flops 3221225472 | bytes 16842752 | tf_op jit(solution)/shard_map/c...ab,cadk->d...kb/dot_general | solution.py:27
  291.7 12.5 fusion.68
  304.2 4.9 copy.186
  309.1 2.8 fusion.378
  313.6 5.1 multiply_subtract_fusion.13
  318.7 8.5 fusion.90
  330.7 12.7 fusion.71
  343.4 4.9 copy.196
  349.2 186.0 %all_to_all.64 = f32[32,4,128,128]{3,2,1,0:T(8,128)} all-to-all(f32[32,4,128,128]{3,2,1,0:T(8,128)S(1)} %fusion.216), channel_id=1, replica_groups=mesh['gx'=8,'gy'=4] {'gx','gy'}, dimensions={0} | all-to-all | bytes 16777216 | tf_op jit(solution)/shard_map/all_to_all | solution.py:67
  535.2 9.0 copy.197
  544.2 15.8 %fusion.74 = f32[2,2,128,64,64]{2,3,4,1,0:T(8,128)S(1)} fusion(f32[2,2,128,64,64]{2,4,3,1,0:T(8,128)} %bitcast.719, f32[1,64,2,64]{1,3,2,0:T(8,128)S(1)} %get-tuple-element.60, f32[1,64,2,64]{1,3,2,0:T(8,128)S(1)} %get-tuple-element.59), kind=kOutput, calls=%fused_computation.115 | convolution fusion | flops 3221241856 | bytes 16842752 | tf_op jit(solution)/shard_map/c...ab,cadk->d...kb/dot_general | solution.py:27
  563.4 12.5 fusion.77
  576.0 4.9 copy.202
  581.2 4.6 convolution_bitcast_fusion.1
  588.2 5.9 fusion.95
  594.1 2.4 copy.206
  596.6 16.1 %copy.207 = f32[2,128,4096]{1,0,2:T(2,128)} copy(f32[2,128,4096]{1,2,0:T(8,128)S(1)} %bitcast.726) | data formatting | bytes 8388608 | tf_op jit(solution)/shard_map/reshape;reshape | solution.py:81
  612.7 4.0 all-to-all-start.2
  625.7 84.6 %all-to-all-done.2 = f32[2,128,4096]{1,0,2:T(2,128)} async-done(((f32[2,128,4096]{1,0,2:T(2,128)}), f32[2,128,4096]{1,0,2:T(2,128)}, u32[]{:S(2)}, u32[]{:S(2)}) %all-to-all-start.2) | async-done | bytes 4194336 | tf_op jit(solution)/shard_map/all_to_all | solution.py:75
  710.4 4.5 copy.208
  714.8 5.7 copy.209
  720.5 8.4 fusion.98
  731.2 6.1 fusion.101
  737.3 10.4 multiply_subtract_fusion.9
  749.3 8.5 fusion.89
  757.9 2.1 multiply_subtract_fusion.1
  761.6 12.5 fusion.80
  774.1 4.9 copy.225
  779.9 187.5 %all_to_all.65 = f32[32,4,128,128]{3,2,1,0:T(8,128)} all-to-all(f32[32,4,128,128]{3,2,1,0:T(8,128)S(1)} %fusion.184), channel_id=1, replica_groups=mesh['gx'=8,'gy'=4] {'gx','gy'}, dimensions={0} | all-to-all | bytes 16777216 | tf_op jit(solution)/shard_map/all_to_all | solution.py:67
  967.4 9.0 copy.226
  976.4 15.8 %fusion.83 = f32[2,2,128,64,64]{2,3,4,1,0:T(8,128)S(1)} fusion(f32[2,2,128,64,64]{2,4,3,1,0:T(8,128)} %bitcast.721, f32[1,64,2,64]{1,3,2,0:T(8,128)S(1)} %get-tuple-element.60, f32[1,64,2,64]{1,3,2,0:T(8,128)S(1)} %get-tuple-element.59), kind=kOutput, calls=%fused_computation.118 | convolution fusion | flops 3221241856 | bytes 16842752 | tf_op jit(solution)/shard_map/c...ab,cadk->d...kb/dot_general | solution.py:27
  992.2 2.0 multiply_subtract_fusion
  995.9 12.5 fusion.86
  1008.3 4.9 copy.231
  1013.6 4.6 convolution_bitcast_fusion
  1020.5 5.9 fusion.104
  1026.3 2.4 copy.235
  1028.8 16.5 %copy.236 = f32[2,128,4096]{1,0,2:T(2,128)} copy(f32[2,128,4096]{1,2,0:T(8,128)S(1)} %bitcast.729) | data formatting | bytes 8388608 | tf_op jit(solution)/shard_map/reshape;reshape | solution.py:81
  1045.3 3.9 all-to-all-start.4
  1049.3 2.5 fusion.379
  1051.8 2.5 copy.244
  1055.6 87.3 %all-to-all-done.4 = f32[2,128,4096]{1,0,2:T(2,128)} async-done(((f32[2,128,4096]{1,0,2:T(2,128)}), f32[2,128,4096]{1,0,2:T(2,128)}, u32[]{:S(2)}, u32[]{:S(2)}) %all-to-all-start.4) | async-done | bytes 4194336 | tf_op jit(solution)/shard_map/all_to_all | solution.py:75
  1142.9 4.5 copy.237
  1147.4 5.7 copy.238
  1153.0 8.4 fusion.107
  1163.6 5.9 fusion.110
  1173.7 5.4 fusion.152
  1179.0 5.3 fusion.156
  1186.0 4.5 fusion.174
  1190.5 2.2 pad_maximum_fusion.6
  1192.8 5.8 copy.246
  1198.6 75.9 %all-gather.2.cloned.1.call-done = f32[2,4096,256]{1,2,0:T(8,128)} async-done(((f32[2,128,256]{1,2,0:T(8,128)}), f32[2,4096,256]{1,2,0:T(8,128)}) %all-gather.2.cloned.1.call-update) | async-done | bytes 8388624 | tf_op jit(solution)/shard_map/all_gather | solution.py:170
  1280.1 1.9 convolution_subtract_fusion
  (145 shorter events, 47.9 us)
Async XLA Ops:
  14.1 1.6 copy-start.5
  62.6 193.7 %all-to-all-start = ((f32[4,128,4096]{1,0,2:T(4,128)}), f32[4,128,4096]{1,0,2:T(4,128)}, u32[]{:S(2)}, u32[]{:S(2)}) async-start(f32[4,128,4096]{1,0,2:T(4,128)} %copy.179), calls=%async_computation | async-start | bytes 16777216 | tf_op jit(solution)/shard_map/all_to_all | solution.py:75
  309.1 4.5 copy-start
  313.6 5.1 copy-start.2
  612.7 4.0 copy-start.10
  612.7 97.7 %all-to-all-start.2 = ((f32[2,128,4096]{1,0,2:T(2,128)}), f32[2,128,4096]{1,0,2:T(2,128)}, u32[]{:S(2)}, u32[]{:S(2)}) async-start(f32[2,128,4096]{1,0,2:T(2,128)} %copy.207), calls=%async_computation.2 | async-start | bytes 8388608 | tf_op jit(solution)/shard_map/all_to_all | solution.py:75
  730.3 0.9 copy-start.9
  731.2 6.1 copy-start.3
  731.2 6.1 copy-start.6
  731.2 6.1 copy-start.7
  737.3 10.4 copy-start.1
  1045.3 97.6 %all-to-all-start.4 = ((f32[2,128,4096]{1,0,2:T(2,128)}), f32[2,128,4096]{1,0,2:T(2,128)}, u32[]{:S(2)}, u32[]{:S(2)}) async-start(f32[2,128,4096]{1,0,2:T(2,128)} %copy.236), calls=%async_computation.4 | async-start | bytes 8388608 | tf_op jit(solution)/shard_map/all_to_all | solution.py:75
  1049.2 225.3 %all-gather.2.cloned.1.call-start = ((), (), s32[]{:S(2)}) async-start(), calls=%async_computation.5 | async-start | bytes 8650752 | tf_op jit(solution)/shard_map/all_gather | solution.py:170
  1169.4 3.1 slice-start
  1170.0 3.0 slice-start.1
  1170.0 3.6 copy-start.4
  1184.4 1.7 copy-start.8
Sparse Core Ops, SparseCore 0:
  1185.2 89.2 all-gather.1
